TPU v7x, 512 devices: a whole 4x4x16 slice. The times are simulated.
512 devices in a mesh: lev: 16 (over x, z_hi, core), hor: 32 (over z_lo, y).
Axes of the slice: x: 4, y: 4, z: 16 (z_hi: 2, z_lo: 8; z = z_hi * 8 + z_lo), core: 2. Of those that a mesh axis runs over, the one named last changes fastest.
Arguments:
- state: float32 [2, 128, 512, 1024], P(None, 'lev', 'hor'), may hold values from -6 to 6
- cotangent: bfloat16 [2, 128, 512, 1024], P(None, 'lev', 'hor'), may hold values from -6 to 6
- diffusion: float32 [128, 512, 1024], P('lev', 'hor'), may hold values from 0.02 to 0.2
- vertical_inverse: float32 [2, 128, 128], replicated, may hold values from -0.2 to 2
- w_in: bfloat16 [1024, 256], replicated, may hold values from -0.375 to 0.375
- w_out: bfloat16 [256, 1024], replicated, may hold values from -0.1875 to 0.1875
Outputs:
- state_adjoint: float32 [2, 128, 512, 1024], P(None, 'lev', 'hor')
All inputs are finite; a program needn't handle non-finite values.
Results may differ from a plain program's by a relative error of at most 0.002.
Values may be sent and summed in bfloat16 or wider, within the bound.
A program may use at most 64 MiB of HBM per device.

v0:
```python
import jax
import jax.numpy as jnp
from jax import lax
from jax.sharding import PartitionSpec as P


def with_halo(block, sides, width):
    for axis, dim in sides:
        count = lax.axis_size(axis)
        forward = [(i, i + 1) for i in range(count - 1)]
        backward = [(target, source) for source, target in forward]
        low = lax.ppermute(
            lax.slice_in_dim(block, block.shape[dim] - width, None, axis=dim), axis, forward
        )
        high = lax.ppermute(lax.slice_in_dim(block, 0, width, axis=dim), axis, backward)
        block = jnp.concatenate([low, block, high], axis=dim)
    return block


def laplace_local(extended):
    padded = jnp.pad(extended, ((0, 0), (0, 0), (0, 0), (1, 1)))
    return (
        padded[:, :, 2:, 1:-1]
        + padded[:, :, :-2, 1:-1]
        + padded[:, :, 1:-1, 2:]
        + padded[:, :, 1:-1, :-2]
        - 4.0 * padded[:, :, 1:-1, 1:-1]
    )


def column_adjoint(diffused, cot_block, vertical_inverse, w_in, w_out):
    highest = lax.Precision.HIGHEST
    solved = jnp.einsum("fkl,flc->fkc", vertical_inverse, diffused, precision=highest)
    fields, levels, count = solved.shape
    inputs = solved.reshape(fields * levels, count).astype(jnp.bfloat16)
    preact = jnp.dot(w_in, inputs, preferred_element_type=jnp.float32)
    cot_cols = cot_block.reshape(fields * levels, count)
    hidden_grad = lax.dot_general(
        w_out, cot_cols, (((0,), (0,)), ((), ())), preferred_element_type=jnp.float32
    )
    squashed = jax.nn.sigmoid(preact)
    pre_grad = (hidden_grad * squashed * (1.0 + preact * (1.0 - squashed))).astype(jnp.bfloat16)
    level_grad = cot_cols.astype(jnp.float32) + lax.dot_general(
        w_in, pre_grad, (((0,), (0,)), ((), ())), preferred_element_type=jnp.float32
    )
    level_grad = level_grad.reshape(fields, levels, count)
    return jnp.einsum("fkl,fkc->flc", vertical_inverse, level_grad, precision=highest)


def body(state, cotangent, diffusion, vertical_inverse, w_in, w_out):
    extended = with_halo(state, (("hor", 2),), 1)
    diffused = state + diffusion[None] * laplace_local(extended)
    state_cols = lax.all_to_all(diffused, "lev", split_axis=3, concat_axis=1, tiled=True)
    cot_cols = lax.all_to_all(cotangent, "lev", split_axis=3, concat_axis=1, tiled=True)
    shape_cols = state_cols.shape
    flat_state = state_cols.reshape(shape_cols[0], shape_cols[1], shape_cols[2] * shape_cols[3])
    flat_cot = cot_cols.reshape(shape_cols[0], shape_cols[1], shape_cols[2] * shape_cols[3])
    adjoint_cols = column_adjoint(flat_state, flat_cot, vertical_inverse, w_in, w_out).reshape(
        shape_cols
    )
    adjoint_levels = lax.all_to_all(adjoint_cols, "lev", split_axis=1, concat_axis=3, tiled=True)
    weighted = diffusion[None] * adjoint_levels
    rimmed = with_halo(weighted, (("hor", 2),), 1)
    return adjoint_levels + laplace_local(rimmed)


def solution(mesh):
    placed = (
        P(None, "lev", "hor", None),
        P(None, "lev", "hor", None),
        P("lev", "hor", None),
        P(),
        P(),
        P(),
    )
    return jax.shard_map(
        body, mesh=mesh, in_specs=placed, out_specs=P(None, "lev", "hor", None), check_vma=False
    )
```

profile of v0, /device:TPU:32, one launch (start us, length us, event | category | flops | bytes accessed | tf_op | source)
XLA Modules:
  0.0 259.4 jit_solution(9660499994656659942)
XLA Ops:
  0.0 0.0 copy-start
  0.0 5.8 %copy.21 = bf16[2,8,16,1024]{2,1,0,3:T(8,128)(2,1)} copy(bf16[2,8,16,1024]{3,2,1,0:T(8,128)(2,1)} %param.7) | data formatting | bytes 1048576 | tf_op args[1]
  5.8 0.0 copy-start.1
  5.8 6.5 %reshape.19 = bf16[16,2,8192]{2,1,0:T(2,128)(2,1)} reshape(bf16[1024,2,8,16]{3,2,1,0:T(8,128)(2,1)} %bitcast.61) | data formatting | bytes 1048576
  12.3 16.8 %all-to-all-start = ((bf16[16,2,8192]{2,1,0:T(2,128)(2,1)}), bf16[16,2,8192]{2,1,0:T(2,128)(2,1)}, u32[]{:S(2)}, u32[]{:S(2)}) async-start(bf16[16,2,8192]{2,1,0:T(2,128)(2,1)} %reshape.19), calls=%async_computation | async-start | bytes 1048576 | tf_op jit(solution)/shard_map/all_to_all | solution.py:54
  29.1 0.0 copy-done.1
  29.1 0.0 copy-start.2
  29.1 0.1 fusion.17
  29.2 5.5 %collective-permute-start = (f32[2,8,1,1024]{3,2,1,0:T(1,128)S(1)}, f32[2,8,1,1024]{3,2,1,0:T(1,128)S(1)}, u32[]{:S(2)}, u32[]{:S(2)}) collective-permute-start(f32[2,8,1,1024]{3,2,1,0:T(1,128)S(1)} %get-tuple-element.8), channel_id=1, source_target_pairs={{1,0},{2,1},{3,2},{4,3},{5,4},{6,5},{7,6},{8,7},{9,8},{10,9},{11,1... | collective-permute-start | bytes 196616 | tf_op jit(solution)/shard_map/ppermute | solution.py:15
  34.7 1.9 collective-permute-start.1
  36.7 17.3 %collective-permute-done = f32[2,8,1,1024]{3,2,1,0:T(1,128)S(1)} collective-permute-done((f32[2,8,1,1024]{3,2,1,0:T(1,128)S(1)}, f32[2,8,1,1024]{3,2,1,0:T(1,128)S(1)}, u32[]{:S(2)}, u32[]{:S(2)}) %collective-permute-start) | collective-permute-done | bytes 65568 | tf_op jit(solution)/shard_map/ppermute | solution.py:15
  53.9 0.0 collective-permute-done.1
  53.9 0.9 select_maximum_fusion.2
  54.8 0.0 copy-done.2
  54.9 0.7 fusion.13
  55.6 6.1 %copy.23 = f32[2,8,16,1024]{2,1,0,3:T(8,128)} copy(f32[2,8,16,1024]{3,2,1,0:T(8,128)S(1)} %fusion.13) | data formatting | bytes 2097152 | tf_op jit(solution)/shard_map/add | solution.py:52
  61.7 7.1 %reshape.17 = f32[16,1,16384]{2,1,0:T(1,128)} reshape(f32[1024,2,8,16]{3,2,1,0:T(8,128)} %bitcast.59) | data formatting | bytes 2097152
  68.9 0.0 all-to-all-done
  68.9 14.2 %all-to-all-start.1 = ((f32[16,1,16384]{2,1,0:T(1,128)}), f32[16,1,16384]{2,1,0:T(1,128)S(1)}, u32[]{:S(2)}, u32[]{:S(2)}) async-start(f32[16,1,16384]{2,1,0:T(1,128)} %reshape.17), calls=%async_computation.1 | async-start | bytes 2097152 | tf_op jit(solution)/shard_map/all_to_all | solution.py:53
  83.0 5.4 %reshape.20 = bf16[1024,2,8,16]{3,2,1,0:T(8,128)(2,1)} reshape(bf16[16,2,8192]{2,1,0:T(2,128)(2,1)} %all-to-all-done) | data formatting | bytes 1048576
  88.4 4.0 %copy.22 = bf16[2,8,16,16,64]{4,2,1,3,0:T(8,128)(2,1)S(1)} copy(bf16[2,8,16,16,64]{2,1,0,4,3:T(8,128)(2,1)} %bitcast.60) | data formatting | bytes 1048576 | tf_op jit(solution)/shard_map/all_to_all | solution.py:54
  92.4 1.6 reshape_reshape.3
  94.0 45.7 %all-to-all-done.1 = f32[16,1,16384]{2,1,0:T(1,128)S(1)} async-done(((f32[16,1,16384]{2,1,0:T(1,128)}), f32[16,1,16384]{2,1,0:T(1,128)S(1)}, u32[]{:S(2)}, u32[]{:S(2)}) %all-to-all-start.1) | async-done | bytes 1048608 | tf_op jit(solution)/shard_map/all_to_all | solution.py:53
  139.7 0.6 broadcast.42
  140.3 3.1 %reduce = f32[16,16384]{1,0:T(8,128)S(1)} reduce(f32[16,1,16384]{2,1,0:T(1,128)S(1)} %all-to-all-done.1, f32[]{:T(128)} %broadcast.42), dimensions={1}, to_apply=%all_to_all.38.reduce_sub_computation | reduce | bytes 2097156 | tf_op jit(solution)/shard_map/all_to_all | solution.py:53
  143.4 4.8 %reshape.18 = f32[1024,2,8,16]{3,2,1,0:T(8,128)} reshape(f32[16,16384]{1,0:T(8,128)S(1)} %reduce) | data formatting | bytes 2097152
  148.2 5.4 %copy.24 = f32[2,8,16,16,64]{4,2,1,3,0:T(8,128)S(1)} copy(f32[2,8,16,16,64]{2,1,0,4,3:T(8,128)} %bitcast.58) | data formatting | bytes 2097152 | tf_op jit(solution)/shard_map/all_to_all | solution.py:53
  153.6 0.0 copy-start.4
  153.6 1.5 reshape.14
  155.2 0.0 copy-done.4
  155.2 2.3 convolution_convert_fusion
  157.4 0.0 copy-done
  157.4 0.0 copy-start.3
  157.5 0.0 copy-start.5
  157.5 2.7 %fusion.19 = f32[1024,1024]{0,1:T(8,128)} fusion(bf16[1024,256]{1,0:T(8,128)(2,1)S(1)} %copy-done, bf16[256,1024]{1,0:T(8,128)(2,1)S(1)} %bitcast.67), kind=kOutput, calls=%fused_computation.38 | convolution fusion | flops 536870912 | bytes 5242880 | tf_op jit(solution)/shard_map/dot_general | solution.py:36
  160.1 0.0 copy-done.3
  160.1 0.0 copy-done.5
  160.1 4.4 %fusion.7 = f32[256,1024]{1,0:T(8,128)S(1)} fusion(bf16[1024,256]{1,0:T(8,128)(2,1)S(1)} %copy-done, f32[1024,1024]{0,1:T(8,128)} %fusion.19, bf16[256,1024]{1,0:T(8,128)(2,1)S(1)} %copy-done.5, bf16[256,1024]{1,0:T(8,128)(2,1)S(1)} %copy-done.3), kind=kOutput, calls=%fused_computation.16 | convolution fusion | flops 1083703296 | bytes 6815744 | tf_op jit(solution)/shard_map/dot_general | solution.py:43
  164.6 2.8 %fusion.18 = f32[2,1024,128]{2,1,0:T(8,128)} fusion(f32[2,128,1024]{2,1,0:T(8,128)S(1)} %bitcast.68, f32[2,128,128]{2,1,0:T(8,128)S(1)} %copy-done.4), kind=kOutput, calls=%fused_computation.37 | convolution fusion | flops 402653184 | bytes 2228224 | tf_op jit(solution)/shard_map/fkl,fkc->flc/dot_general | solution.py:47
  167.3 3.1 %copy.27 = f32[2,128,16,64]{3,2,0,1:T(8,128)S(1)} copy(f32[2,128,16,64]{1,3,2,0:T(8,128)} %bitcast.66) | data formatting | bytes 2097152 | tf_op jit(solution)/shard_map/reshape | solution.py:58
  170.4 2.3 reshape.21
  172.7 62.7 %all_to_all.48 = f32[16,1,16384]{2,1,0:T(1,128)S(1)} all-to-all(f32[16,1,16384]{2,1,0:T(1,128)} %reshape.21), channel_id=1, replica_groups=mesh['lev'=16,'hor'=32] {'lev'}, dimensions={0} | all-to-all | bytes 2097152 | tf_op jit(solution)/shard_map/all_to_all | solution.py:61
  235.4 4.4 %reduce.1 = f32[16,16384]{1,0:T(8,128)} reduce(f32[16,1,16384]{2,1,0:T(1,128)S(1)} %all_to_all.48, f32[]{:T(128)} %broadcast.42), dimensions={1}, to_apply=%all_to_all.41.reduce_sub_computation | reduce | bytes 2097156 | tf_op jit(solution)/shard_map/all_to_all | solution.py:61
  239.7 2.1 reshape.22
  241.8 2.6 copy.29
  244.3 2.0 all_to_all.44
  246.4 0.1 broadcast_multiply_fusion
  246.5 0.1 fusion.16
  246.6 1.9 collective-permute-start.2
  248.5 3.9 %collective-permute-start.3 = (f32[2,8,1,1024]{3,2,1,0:T(1,128)S(1)}, f32[2,8,1,1024]{3,2,1,0:T(1,128)S(1)}, u32[]{:S(2)}, u32[]{:S(2)}) collective-permute-start(f32[2,8,1,1024]{3,2,1,0:T(1,128)S(1)} %get-tuple-element.5), channel_id=1, source_target_pairs={{0,1},{1,2},{2,3},{3,4},{4,5},{5,6},{6,7},{7,8},{8,9},{9,10},{10,1... | collective-permute-start | bytes 196616 | tf_op jit(solution)/shard_map/ppermute | solution.py:12
  252.4 0.3 collective-permute-done.2
  252.7 4.0 %collective-permute-done.3 = f32[2,8,1,1024]{3,2,1,0:T(1,128)S(1)} collective-permute-done((f32[2,8,1,1024]{3,2,1,0:T(1,128)S(1)}, f32[2,8,1,1024]{3,2,1,0:T(1,128)S(1)}, u32[]{:S(2)}, u32[]{:S(2)}) %collective-permute-start.3) | collective-permute-done | bytes 65568 | tf_op jit(solution)/shard_map/ppermute | solution.py:12
  256.8 0.9 select_maximum_fusion
  257.7 1.7 fusion.9
Async XLA Ops:
  0.0 157.4 %copy-start = (bf16[1024,256]{1,0:T(8,128)(2,1)S(1)}, bf16[1024,256]{1,0:T(8,128)(2,1)}, u32[]{:S(2)}) copy-start(bf16[1024,256]{1,0:T(8,128)(2,1)} %param.10) | copy-start | bytes 1572868
  5.8 23.3 %copy-start.1 = (f32[2,8,16,1024]{3,2,1,0:T(8,128)S(1)}, f32[2,8,16,1024]{3,2,1,0:T(8,128)}, u32[]{:S(2)}) copy-start(f32[2,8,16,1024]{3,2,1,0:T(8,128)} %param.6) | copy-start | bytes 3145732
  12.3 56.6 %all-to-all-start = ((bf16[16,2,8192]{2,1,0:T(2,128)(2,1)}), bf16[16,2,8192]{2,1,0:T(2,128)(2,1)}, u32[]{:S(2)}, u32[]{:S(2)}) async-start(bf16[16,2,8192]{2,1,0:T(2,128)(2,1)} %reshape.19), calls=%async_computation | async-start | bytes 1048576 | tf_op jit(solution)/shard_map/all_to_all | solution.py:54
  29.1 25.7 %copy-start.2 = (f32[8,16,1024]{2,1,0:T(8,128)S(1)}, f32[8,16,1024]{2,1,0:T(8,128)}, u32[]{:S(2)}) copy-start(f32[8,16,1024]{2,1,0:T(8,128)} %param.8) | copy-start | bytes 1572868
  29.2 24.7 %collective-permute-start = (f32[2,8,1,1024]{3,2,1,0:T(1,128)S(1)}, f32[2,8,1,1024]{3,2,1,0:T(1,128)S(1)}, u32[]{:S(2)}, u32[]{:S(2)}) collective-permute-start(f32[2,8,1,1024]{3,2,1,0:T(1,128)S(1)} %get-tuple-element.8), channel_id=1, source_target_pairs={{1,0},{2,1},{3,2},{4,3},{5,4},{6,5},{7,6},{8,7},{9,8},{10,9},{11,1... | collective-permute-start | bytes 196616 | tf_op jit(solution)/shard_map/ppermute | solution.py:15
  34.7 19.2 %collective-permute-start.1 = (f32[2,8,1,1024]{3,2,1,0:T(1,128)S(1)}, f32[2,8,1,1024]{3,2,1,0:T(1,128)S(1)}, u32[]{:S(2)}, u32[]{:S(2)}) collective-permute-start(f32[2,8,1,1024]{3,2,1,0:T(1,128)S(1)} %get-tuple-element.7), channel_id=1, source_target_pairs={{0,1},{1,2},{2,3},{3,4},{4,5},{5,6},{6,7},{7,8},{8,9},{9,10},{10,1... | collective-permute-start | bytes 196616 | tf_op jit(solution)/shard_map/ppermute | solution.py:12
  68.9 70.9 %all-to-all-start.1 = ((f32[16,1,16384]{2,1,0:T(1,128)}), f32[16,1,16384]{2,1,0:T(1,128)S(1)}, u32[]{:S(2)}, u32[]{:S(2)}) async-start(f32[16,1,16384]{2,1,0:T(1,128)} %reshape.17), calls=%async_computation.1 | async-start | bytes 2097152 | tf_op jit(solution)/shard_map/all_to_all | solution.py:53
  153.6 1.6 copy-start.4
  157.4 2.7 %copy-start.3 = (bf16[256,1024]{1,0:T(8,128)(2,1)S(1)}, bf16[256,1024]{1,0:T(8,128)(2,1)}, u32[]{:S(2)}) copy-start(bf16[256,1024]{1,0:T(8,128)(2,1)} %reshape_reshape.3) | copy-start | bytes 1572868
  157.5 2.7 %copy-start.5 = (bf16[256,1024]{1,0:T(8,128)(2,1)S(1)}, bf16[256,1024]{1,0:T(8,128)(2,1)}, u32[]{:S(2)}) copy-start(bf16[256,1024]{1,0:T(8,128)(2,1)} %param.11) | copy-start | bytes 1572868
  246.6 6.2 %collective-permute-start.2 = (f32[2,8,1,1024]{3,2,1,0:T(1,128)S(1)}, f32[2,8,1,1024]{3,2,1,0:T(1,128)S(1)}, u32[]{:S(2)}, u32[]{:S(2)}) collective-permute-start(f32[2,8,1,1024]{3,2,1,0:T(1,128)S(1)} %get-tuple-element.6), channel_id=1, source_target_pairs={{1,0},{2,1},{3,2},{4,3},{5,4},{6,5},{7,6},{8,7},{9,8},{10,9},{11,1... | collective-permute-start | bytes 196616 | tf_op jit(solution)/shard_map/ppermute | solution.py:15
  248.5 8.3 %collective-permute-start.3 = (f32[2,8,1,1024]{3,2,1,0:T(1,128)S(1)}, f32[2,8,1,1024]{3,2,1,0:T(1,128)S(1)}, u32[]{:S(2)}, u32[]{:S(2)}) collective-permute-start(f32[2,8,1,1024]{3,2,1,0:T(1,128)S(1)} %get-tuple-element.5), channel_id=1, source_target_pairs={{0,1},{1,2},{2,3},{3,4},{4,5},{5,6},{6,7},{7,8},{8,9},{9,10},{10,1... | collective-permute-start | bytes 196616 | tf_op jit(solution)/shard_map/ppermute | solution.py:12
where the time goes:
time: 260 us; the launch traced here: 259 us
  waiting for transfers between devices  67.3 us (26%)
  blocking collectives  62.7 us (24%)
  local copies, waits for them, and re-layouts  60.9 us (23%)
  starting transfers between devices  44.2 us (17%)
  matrix products  12.1 us (5%)
  other arithmetic  11.8 us (5%)
    all_to_all x1, blocking collectives, body(): lax.all_to_all(adjoint_cols, 'lev', split_axis=1, concat_axis=3, tiled=True)  62.7 us
    all_to_all x1, waiting for transfers between devices, body(): lax.all_to_all(diffused, 'lev', split_axis=3, concat_axis=1, tiled=True)  45.7 us
    unnamed x19, local copies, waits for them, and re-layouts  33.9 us
    ppermute x2, waiting for transfers between devices, with_halo(): lax.ppermute(lax.slice_in_dim(block, 0, width, axis=dim), axis, backward)  17.6 us
    all_to_all x1, starting transfers between devices, body(): lax.all_to_all(cotangent, 'lev', split_axis=3, concat_axis=1, tiled=True)  16.8 us
    all_to_all x1, starting transfers between devices, body(): lax.all_to_all(diffused, 'lev', split_axis=3, concat_axis=1, tiled=True)  14.2 us
    ppermute x2, starting transfers between devices, with_halo(): lax.ppermute(lax.slice_in_dim(block, 0, width, axis=dim), axis, backward)  7.42 us
    add x1, local copies, waits for them, and re-layouts, body(): diffused = state + diffusion[None] * laplace_local(extended)  6.14 us
  transfers between devices with their start and end apart: 6, of which 4 were waited for; matrix products, arithmetic and copies ran while one was open for 10% of the time, Pallas kernels for 0%

commit v1 on v0

v1 whole, which is shorter than its diff:
```python
import functools

import jax
import jax.numpy as jnp
from jax import lax
from jax.experimental import pallas as pl
from jax.experimental.pallas import tpu as pltpu
from jax.sharding import PartitionSpec as P

MESH = pl.DeviceIdType.MESH
F32 = jnp.float32
BF16 = jnp.bfloat16
CHUNKS = 4
COLS = 1024
WIDE = COLS // CHUNKS
LEVS = 16
ROWS = 16
HID = 1024
TILES = COLS // 128


def nt(a, b):
    return lax.dot_general(a, b, (((1,), (1,)), ((), ())), preferred_element_type=F32)


def nn(a, b):
    return jnp.dot(a, b, preferred_element_type=F32)


def sides_of(block):
    lane = lax.broadcasted_iota(jnp.int32, block.shape, 1)
    left = jnp.where(lane == 0, 0.0, pltpu.roll(block, 1, 1))
    right = jnp.where(lane == block.shape[1] - 1, 0.0, pltpu.roll(block, block.shape[1] - 1, 1))
    return left + right


def kernel(
    state_hbm, cot_hbm, diff_hbm, vinv_hbm, w_in_hbm, w_out_hbm, out_hbm,
    state_v, cot_v, diff_v, vinv_v, w_in_v, w_out_v, out_v,
    cot_f, grid_s, grid_w, adj_v,
    s_cot, r_cot, s_state, r_state, s_adj, r_adj,
    w_in_p, w_in_t, w_out_t, v_fwd, v_adj, gain,
    in_sems, tile_sems, cot_sems, state_sems, adj_sems, halo_a, halo_b,
):
    me = lax.axis_index("lev")
    hor = lax.axis_index("hor")
    last = lax.axis_size("hor") - 1

    def tiles(wide, tall, sem, out=False):
        pairs = [(wide.at[:, pl.ds(t * 128, 128)], tall.at[t]) for t in range(TILES)]
        return [pltpu.make_async_copy(b, a, sem.at[t]) if out else pltpu.make_async_copy(a, b, sem.at[t])
                for t, (a, b) in enumerate(pairs)]

    cot_load = pltpu.make_async_copy(cot_hbm, cot_v, in_sems.at[0])
    state_load = tiles(state_hbm, state_v, tile_sems.at[0])
    rest = tiles(diff_hbm, diff_v, tile_sems.at[1]) + [
        pltpu.make_async_copy(src, dst, in_sems.at[i + 1])
        for i, (src, dst) in enumerate(((vinv_hbm, vinv_v), (w_in_hbm, w_in_v), (w_out_hbm, w_out_v)))
    ]
    loads = [cot_load] + state_load + rest
    for load in loads:
        load.start()

    barrier = pltpu.get_barrier_semaphore()

    @pl.loop(1, LEVS)
    def _(j):
        pl.semaphore_signal(
            barrier, inc=1, device_id={"lev": lax.rem(me + j, LEVS), "hor": hor}, device_id_type=MESH
        )

    @pl.when(hor > 0)
    def _():
        pl.semaphore_signal(barrier, inc=1, device_id={"lev": me, "hor": hor - 1}, device_id_type=MESH)

    @pl.when(hor < last)
    def _():
        pl.semaphore_signal(barrier, inc=1, device_id={"lev": me, "hor": hor + 1}, device_id_type=MESH)

    def across(ref, base, lo=0, hi=COLS):
        return jnp.concatenate(
            [ref[t, pl.ds(base, 8, stride=ROWS), :] for t in range(lo // 128, hi // 128)], axis=1
        )

    def both(ref, r):
        return jnp.concatenate([across(ref, r), across(ref, 128 + r)], axis=0)

    def doubled(ref, r, lo=0, hi=COLS):
        coef = across(ref, r, lo, hi)
        return jnp.concatenate([coef, coef], axis=0)

    cot_load.wait()
    for t in range(TILES):
        cot_f[t] = cot_v[:, t * 128:(t + 1) * 128].astype(F32)

    @pl.loop(0, ROWS)
    def _(r):
        row = both(cot_f, r).astype(BF16)
        for c in range(CHUNKS):
            s_cot[c, r] = row[:, c * WIDE:(c + 1) * WIDE]

    for c in range(CHUNKS):
        r_cot[c, me] = s_cot[c, me]

    for load in state_load:
        load.wait()

    @pl.loop(0, ROWS)
    def _(r):
        grid_s[r + 1] = both(state_v, r)

    @pl.when(hor == 0)
    def _():
        grid_s[0] = jnp.zeros((16, COLS), F32)
        grid_w[0] = jnp.zeros((16, COLS), F32)

    @pl.when(hor == last)
    def _():
        grid_s[ROWS + 1] = jnp.zeros((16, COLS), F32)
        grid_w[ROWS + 1] = jnp.zeros((16, COLS), F32)

    for load in rest:
        load.wait()

    pl.semaphore_wait(
        barrier, LEVS - 1 + (hor > 0).astype(jnp.int32) + (hor < last).astype(jnp.int32)
    )

    def edge(grid, sems, up, cols):
        src, dst = (ROWS, 0) if up else (1, ROWS + 1)
        return pltpu.make_async_remote_copy(
            src_ref=grid.at[src, :, cols], dst_ref=grid.at[dst, :, cols],
            send_sem=sems.at[0, int(up)], recv_sem=sems.at[1, int(up)],
            device_id={"lev": me, "hor": hor + (1 if up else -1)}, device_id_type=MESH,
        )

    def swap_start(grid, sems, cols):
        @pl.when(hor > 0)
        def _():
            edge(grid, sems, False, cols).start()

        @pl.when(hor < last)
        def _():
            edge(grid, sems, True, cols).start()

    def swap_wait(grid, sems, cols):
        @pl.when(hor > 0)
        def _():
            edge(grid, sems, False, cols).wait_send()
            edge(grid, sems, True, cols).wait_recv()

        @pl.when(hor < last)
        def _():
            edge(grid, sems, True, cols).wait_send()
            edge(grid, sems, False, cols).wait_recv()

    def spread(src, dst, sems, c):
        @pl.loop(1, LEVS)
        def _(j):
            peer = lax.rem(me + j, LEVS)
            pltpu.make_async_remote_copy(
                src_ref=src.at[c, peer], dst_ref=dst.at[c, me],
                send_sem=sems.at[0, c], recv_sem=sems.at[1, c],
                device_id={"lev": peer, "hor": hor}, device_id_type=MESH,
            ).start()

    def gathered(buf, sems, way, c):
        part = buf.at[c, pl.ds(0, LEVS - 1)]
        pltpu.make_async_copy(part, part, sems.at[way, c]).wait()

    full = pl.ds(0, COLS)
    swap_start(grid_s, halo_a, full)
    for c in range(CHUNKS):
        spread(s_cot, r_cot, cot_sems, c)

    swap_wait(grid_s, halo_a, full)

    @pl.loop(0, ROWS)
    def _(r):
        mid = grid_s[r + 1]
        around = grid_s[r] + grid_s[r + 2] + sides_of(mid) - 4.0 * mid
        row = (mid + doubled(diff_v, r) * around).astype(BF16)
        for c in range(CHUNKS):
            s_state[c, r] = row[:, c * WIDE:(c + 1) * WIDE]

    for c in range(CHUNKS):
        spread(s_state, r_state, state_sems, c)
    for c in range(CHUNKS):
        r_state[c, me] = s_state[c, me]

    at_p = lax.broadcasted_iota(jnp.int32, (256, 256), 0)
    at_k = lax.broadcasted_iota(jnp.int32, (256, 256), 1)
    place = (at_p // 16) * 8 + (at_p % 16) // 8 * 128 + at_p % 8
    perm_t = (place == at_k).astype(F32).astype(BF16)
    w_in_p[...] = nt(w_in_v[...], perm_t).astype(BF16)
    w_in_t[...] = nt(perm_t, w_in_v[...]).astype(BF16)
    w_out_t[...] = nn(perm_t, w_out_v[...]).T.astype(BF16)
    eye = lax.broadcasted_iota(jnp.int32, (128, 128), 0) == lax.broadcasted_iota(jnp.int32, (128, 128), 1)
    parts = [jnp.zeros((256, 256), F32) for _ in range(2)]
    for f in range(2):
        exact = vinv_v[f]
        high = exact.astype(BF16)
        low = (exact - high.astype(F32)).astype(BF16)
        sel = perm_t[:, f * 128:(f + 1) * 128]
        for i, piece in enumerate((high, low)):
            parts[i] += nn(sel, nt(piece, sel).astype(BF16))
        diag = jnp.sum(jnp.where(eye, exact, 0.0), axis=1, keepdims=True)
        for src in range(LEVS):
            gain[src * 16 + f * 8:src * 16 + f * 8 + 8, :] = jnp.broadcast_to(
                diag[src * 8:src * 8 + 8], (8, 128)
            )
    for i in range(2):
        v_fwd[:, i * 256:(i + 1) * 256] = parts[i].astype(BF16)
    high_t = parts[0].T.astype(BF16)
    v_adj[:, 0:256] = high_t
    v_adj[:, 256:512] = high_t
    v_adj[:, 512:768] = parts[1].T.astype(BF16)

    def columns(c):
        diffused = r_state[c].reshape(256, WIDE)
        cot = r_cot[c].reshape(256, WIDE)
        solved = nn(v_fwd[...], jnp.concatenate([diffused, diffused], axis=0))
        inputs = solved.astype(BF16)
        level = cot.astype(F32)
        for h in range(4):
            hs = slice(h * 256, (h + 1) * 256)
            preact = nn(w_in_p[hs, :], inputs)
            hidden = nn(w_out_t[hs, :], cot)
            s = 0.5 + 0.5 * jnp.tanh(0.5 * preact)
            pre = (hidden * s * (1.0 + preact * (1.0 - s))).astype(BF16)
            level = level + nn(w_in_t[:, hs], pre)
        high = level.astype(BF16)
        low = (level - high.astype(F32)).astype(BF16)
        adjoint = nn(v_adj[...], jnp.concatenate([high, low, high], axis=0))
        delta = adjoint - gain[:, 0:1] * cot.astype(F32)
        s_adj[c] = delta.astype(BF16).reshape(LEVS, 16, WIDE)

    @pl.loop(0, CHUNKS)
    def _(c):
        gathered(r_cot, cot_sems, 1, c)
        gathered(r_state, state_sems, 1, c)
        columns(c)
        spread(s_adj, r_adj, adj_sems, c)
        r_adj[c, me] = s_adj[c, me]

    scale = gain[pl.ds(pl.multiple_of(me * 16, 16), 16), 0:1]
    for c in range(CHUNKS):
        gathered(r_adj, adj_sems, 1, c)
        cols = slice(c * WIDE, (c + 1) * WIDE)

        @pl.loop(0, ROWS)
        def _(r):
            adj = r_adj[c, r].astype(F32) + scale * s_cot[c, r].astype(F32)
            adj_v[r, :, cols] = adj
            grid_w[r + 1, :, cols] = doubled(diff_v, r, c * WIDE, (c + 1) * WIDE) * adj

        swap_start(grid_w, halo_b.at[c], pl.ds(c * WIDE, WIDE))
    for c in range(CHUNKS):
        swap_wait(grid_w, halo_b.at[c], pl.ds(c * WIDE, WIDE))

    @pl.loop(0, ROWS)
    def _(r):
        mid = grid_w[r + 1]
        row = adj_v[r] + (grid_w[r] + grid_w[r + 2] + sides_of(mid) - 4.0 * mid)
        for t in range(TILES):
            out_v[t, pl.ds(r, 8, stride=ROWS), :] = row[0:8, t * 128:(t + 1) * 128]
            out_v[t, pl.ds(128 + r, 8, stride=ROWS), :] = row[8:16, t * 128:(t + 1) * 128]

    stores = tiles(out_hbm, out_v, tile_sems.at[2], out=True)
    for store in stores:
        store.start()
    for c in range(CHUNKS):
        gathered(s_cot, cot_sems, 0, c)
        gathered(s_state, state_sems, 0, c)
        gathered(s_adj, adj_sems, 0, c)
    for store in stores:
        store.wait()


def body(state, cotangent, diffusion, vertical_inverse, w_in, w_out):
    dma = pltpu.SemaphoreType.DMA
    slabs = (CHUNKS, LEVS, 16, WIDE)
    out = pl.pallas_call(
        kernel,
        out_shape=jax.ShapeDtypeStruct((256, COLS), F32),
        in_specs=[pl.BlockSpec(memory_space=pltpu.HBM)] * 6,
        out_specs=pl.BlockSpec(memory_space=pl.ANY),
        scratch_shapes=[
            pltpu.VMEM((TILES, 256, 128), F32), pltpu.VMEM((256, COLS), BF16), pltpu.VMEM((TILES, 128, 128), F32),
            pltpu.VMEM((2, 128, 128), F32), pltpu.VMEM((HID, 256), BF16), pltpu.VMEM((256, HID), BF16),
            pltpu.VMEM((TILES, 256, 128), F32),
            pltpu.VMEM((TILES, 256, 128), F32), pltpu.VMEM((ROWS + 2, 16, COLS), F32),
            pltpu.VMEM((ROWS + 2, 16, COLS), F32), pltpu.VMEM((ROWS, 16, COLS), F32),
        ] + [pltpu.VMEM(slabs, BF16)] * 6 + [
            pltpu.VMEM((HID, 256), BF16), pltpu.VMEM((256, HID), BF16), pltpu.VMEM((HID, 256), BF16),
            pltpu.VMEM((256, 512), BF16), pltpu.VMEM((256, 768), BF16), pltpu.VMEM((256, 128), F32),
            dma((4,)), dma((3, TILES)), dma((2, CHUNKS)), dma((2, CHUNKS)), dma((2, CHUNKS)), dma((2, 2)), dma((CHUNKS, 2, 2)),
        ],
        compiler_params=pltpu.CompilerParams(
            collective_id=0, has_side_effects=True, vmem_limit_bytes=48 << 20
        ),
    )(
        state.reshape(256, COLS), cotangent.reshape(256, COLS), diffusion.reshape(128, COLS),
        vertical_inverse, w_in, w_out,
    )
    return out.reshape(2, 8, ROWS, COLS)


def solution(mesh):
    placed = (
        P(None, "lev", "hor", None),
        P(None, "lev", "hor", None),
        P("lev", "hor", None),
        P(),
        P(),
        P(),
    )
    return jax.shard_map(
        body, mesh=mesh, in_specs=placed, out_specs=P(None, "lev", "hor", None), check_vma=False
    )
```

time: 260 us -> 112 us (0.43)
  the two profiles are of different devices: /device:TPU:32 before, /device:TPU:384 now
where the time goes in v1:
time: 112 us
  Pallas kernels  104 us (93%)
  local copies, waits for them, and re-layouts  7.26 us (6%)
    pallas_call x1, Pallas kernels, body(): pl.pallas_call(kernel, out_shape=jax.ShapeDtypeStruct((256, COLS), F32),...  104 us
    unnamed x13, local copies, waits for them, and re-layouts  7.26 us

profile of v1, /device:TPU:384, one launch (start us, length us, event | category | flops | bytes accessed | tf_op | source)
XLA Modules:
  0.0 111.8 jit_solution(13224530730902439962)
XLA Ops:
  0.0 0.0 copy-start
  0.0 1.2 %copy-done = f32[2,8,16,1024]{3,2,1,0:T(8,128)S(1)} copy-done((f32[2,8,16,1024]{3,2,1,0:T(8,128)S(1)}, f32[2,8,16,1024]{3,2,1,0:T(8,128)}, u32[]{:S(2)}) %copy-start) | copy-done | bytes 1048600
  1.2 0.0 copy-start.1
  1.2 1.0 copy-done.1
  2.3 0.0 copy-start.2
  2.3 1.0 copy-done.2
  3.3 0.0 copy-start.3
  3.3 1.0 copy-done.3
  4.4 0.0 copy-start.4
  4.4 1.0 copy-done.4
  5.4 0.0 copy-start.5
  5.4 0.9 copy-done.5
  6.3 104.5 %shard_map.64 = f32[256,1024]{1,0:T(8,128)S(1)} custom-call(f32[256,1024]{1,0:T(8,128)S(1)} %bitcast.5, bf16[256,1024]{1,0:T(8,128)(2,1)S(1)} %bitcast.6, f32[128,1024]{1,0:T(8,128)S(1)} %bitcast.7, f32[2,128,128]{2,1,0:T(8,128)S(1)} %copy-done.5, bf16[1024,256]{1,0:T(8,128)(2,1)S(1)} %copy-done.3, bf16[256,1024]{1,0:T(8,128)(2,1)S(1)} %copy-done.4), custom_call_target="tpu_custom_call" | custom-call | tf_op jit(solution)/shard_map/pallas_call | solution.py:283
  110.8 1.0 copy.8
Async XLA Ops:
  0.0 1.2 %copy-start = (f32[2,8,16,1024]{3,2,1,0:T(8,128)S(1)}, f32[2,8,16,1024]{3,2,1,0:T(8,128)}, u32[]{:S(2)}) copy-start(f32[2,8,16,1024]{3,2,1,0:T(8,128)} %param.6) | copy-start | bytes 3145732
  1.2 1.0 copy-start.1
  2.3 1.0 copy-start.2
  3.3 1.0 copy-start.3
  4.4 1.0 copy-start.4
  5.4 0.9 copy-start.5

commit v2 on v1

--- a/solution.py
+++ b/solution.py
@@ -282,9 +282,9 @@
     slabs = (CHUNKS, LEVS, 16, WIDE)
     out = pl.pallas_call(
         kernel,
-        out_shape=jax.ShapeDtypeStruct((256, COLS), F32),
+        out_shape=pltpu.VMEM((256, COLS), F32),
         in_specs=[pl.BlockSpec(memory_space=pltpu.HBM)] * 6,
-        out_specs=pl.BlockSpec(memory_space=pl.ANY),
+        out_specs=pl.BlockSpec(memory_space=pltpu.VMEM),
         scratch_shapes=[
             pltpu.VMEM((TILES, 256, 128), F32), pltpu.VMEM((256, COLS), BF16), pltpu.VMEM((TILES, 128, 128), F32),
             pltpu.VMEM((2, 128, 128), F32), pltpu.VMEM((HID, 256), BF16), pltpu.VMEM((256, HID), BF16),
@@ -297,12 +297,13 @@
             dma((4,)), dma((3, TILES)), dma((2, CHUNKS)), dma((2, CHUNKS)), dma((2, CHUNKS)), dma((2, 2)), dma((CHUNKS, 2, 2)),
         ],
         compiler_params=pltpu.CompilerParams(
-            collective_id=0, has_side_effects=True, vmem_limit_bytes=48 << 20
+            collective_id=0, has_side_effects=True, vmem_limit_bytes=44 << 20
         ),
-    )(
-        state.reshape(256, COLS), cotangent.reshape(256, COLS), diffusion.reshape(128, COLS),
-        vertical_inverse, w_in, w_out,
-    )
+    )(*[
+        pltpu.with_memory_space_constraint(x, pltpu.HBM)
+        for x in (state.reshape(256, COLS), cotangent.reshape(256, COLS), diffusion.reshape(128, COLS),
+                  vertical_inverse, w_in, w_out)
+    ])
     return out.reshape(2, 8, ROWS, COLS)
 
 

time: 112 us -> 99.5 us (0.89)
  the two profiles are of different devices: /device:TPU:384 before, /device:TPU:32 now
where the time goes in v2:
time: 99.5 us; the launch traced here: 99.2 us
  Pallas kernels  98.2 us (99%)
    pallas_call x1, Pallas kernels, body(): pl.pallas_call(kernel, out_shape=pltpu.VMEM((256, COLS), F32), in_specs=[...  98.2 us

profile of v2, /device:TPU:32, one launch (start us, length us, event | category | flops | bytes accessed | tf_op | source)
XLA Modules:
  0.0 99.2 jit_solution(16296403071669291438)
XLA Ops:
  0.0 98.2 %shard_map.64 = f32[256,1024]{1,0:T(8,128)S(1)} custom-call(f32[256,1024]{1,0:T(8,128)} %bitcast.5, bf16[256,1024]{1,0:T(8,128)(2,1)} %bitcast.6, f32[128,1024]{1,0:T(8,128)} %bitcast.7, f32[2,128,128]{2,1,0:T(8,128)} %vinv_hbm.1, bf16[1024,256]{1,0:T(8,128)(2,1)} %w_in_hbm.1, bf16[256,1024]{1,0:T(8,128)(2,1)} %w_out_hbm.1), custom_call_target="tpu_custom_call" | custom-call | tf_op jit(solution)/shard_map/pallas_call | solution.py:283
  98.2 1.0 copy.8

commit v3 on v2

--- a/solution.py
+++ b/solution.py
@@ -77,6 +77,19 @@
     def _():
         pl.semaphore_signal(barrier, inc=1, device_id={"lev": me, "hor": hor + 1}, device_id_type=MESH)
 
+    def slot(r):
+        depth = jnp.minimum(r, ROWS - 1 - r)
+        return depth // 2, lax.rem(depth, 2) * 8 + (r >= ROWS // 2).astype(jnp.int32) * 4
+
+    def put(buf, r, row):
+        c, first = slot(r)
+        for i in range(4):
+            buf[c, first + i] = row[:, i * WIDE:(i + 1) * WIDE]
+
+    def take(buf, r):
+        c, first = slot(r)
+        return jnp.concatenate([buf[c, first + i] for i in range(4)], axis=1).astype(F32)
+
     def across(ref, base, lo=0, hi=COLS):
         return jnp.concatenate(
             [ref[t, pl.ds(base, 8, stride=ROWS), :] for t in range(lo // 128, hi // 128)], axis=1
@@ -95,9 +108,7 @@
 
     @pl.loop(0, ROWS)
     def _(r):
-        row = both(cot_f, r).astype(BF16)
-        for c in range(CHUNKS):
-            s_cot[c, r] = row[:, c * WIDE:(c + 1) * WIDE]
+        put(s_cot, r, both(cot_f, r).astype(BF16))
 
     for c in range(CHUNKS):
         r_cot[c, me] = s_cot[c, me]
@@ -179,9 +190,7 @@
     def _(r):
         mid = grid_s[r + 1]
         around = grid_s[r] + grid_s[r + 2] + sides_of(mid) - 4.0 * mid
-        row = (mid + doubled(diff_v, r) * around).astype(BF16)
-        for c in range(CHUNKS):
-            s_state[c, r] = row[:, c * WIDE:(c + 1) * WIDE]
+        put(s_state, r, (mid + doubled(diff_v, r) * around).astype(BF16))
 
     for c in range(CHUNKS):
         spread(s_state, r_state, state_sems, c)
@@ -244,27 +253,34 @@
         r_adj[c, me] = s_adj[c, me]
 
     scale = gain[pl.ds(pl.multiple_of(me * 16, 16), 16), 0:1]
-    for c in range(CHUNKS):
-        gathered(r_adj, adj_sems, 1, c)
-        cols = slice(c * WIDE, (c + 1) * WIDE)
-
-        @pl.loop(0, ROWS)
-        def _(r):
-            adj = r_adj[c, r].astype(F32) + scale * s_cot[c, r].astype(F32)
-            adj_v[r, :, cols] = adj
-            grid_w[r + 1, :, cols] = doubled(diff_v, r, c * WIDE, (c + 1) * WIDE) * adj
-
-        swap_start(grid_w, halo_b.at[c], pl.ds(c * WIDE, WIDE))
-    for c in range(CHUNKS):
-        swap_wait(grid_w, halo_b.at[c], pl.ds(c * WIDE, WIDE))
-
-    @pl.loop(0, ROWS)
-    def _(r):
+
+    def stencil(r):
         mid = grid_w[r + 1]
         row = adj_v[r] + (grid_w[r] + grid_w[r + 2] + sides_of(mid) - 4.0 * mid)
         for t in range(TILES):
             out_v[t, pl.ds(r, 8, stride=ROWS), :] = row[0:8, t * 128:(t + 1) * 128]
             out_v[t, pl.ds(128 + r, 8, stride=ROWS), :] = row[8:16, t * 128:(t + 1) * 128]
+
+    def mirrored(start, stop, one):
+        @pl.loop(start, stop)
+        def _(r):
+            one(r)
+            one(ROWS - 1 - r)
+
+    def weigh(r):
+        adj = take(r_adj, r) + scale * take(s_cot, r)
+        adj_v[r] = adj
+        grid_w[r + 1] = doubled(diff_v, r) * adj
+
+    for c in range(CHUNKS):
+        gathered(r_adj, adj_sems, 1, c)
+        mirrored(2 * c, 2 * c + 2, weigh)
+        if c == 0:
+            swap_start(grid_w, halo_b, full)
+        if c == CHUNKS - 2:
+            swap_wait(grid_w, halo_b, full)
+            mirrored(0, 1, stencil)
+        mirrored(max(1, 2 * c - 1), 2 * c + (2 if c == CHUNKS - 1 else 1), stencil)
 
     stores = tiles(out_hbm, out_v, tile_sems.at[2], out=True)
     for store in stores:
@@ -294,7 +310,7 @@
         ] + [pltpu.VMEM(slabs, BF16)] * 6 + [
             pltpu.VMEM((HID, 256), BF16), pltpu.VMEM((256, HID), BF16), pltpu.VMEM((HID, 256), BF16),
             pltpu.VMEM((256, 512), BF16), pltpu.VMEM((256, 768), BF16), pltpu.VMEM((256, 128), F32),
-            dma((4,)), dma((3, TILES)), dma((2, CHUNKS)), dma((2, CHUNKS)), dma((2, CHUNKS)), dma((2, 2)), dma((CHUNKS, 2, 2)),
+            dma((4,)), dma((3, TILES)), dma((2, CHUNKS)), dma((2, CHUNKS)), dma((2, CHUNKS)), dma((2, 2)), dma((2, 2)),
         ],
         compiler_params=pltpu.CompilerParams(
             collective_id=0, has_side_effects=True, vmem_limit_bytes=44 << 20

time: 99.5 us -> 96.8 us (0.973)
  the two profiles are of different devices: /device:TPU:32 before, /device:TPU:193 now
where the time goes in v3:
time: 96.8 us; the launch traced here: 96.7 us
  Pallas kernels  95.7 us (99%)
  local copies, waits for them, and re-layouts  0.97 us (1%)
    pallas_call x1, Pallas kernels, body(): pl.pallas_call(kernel, out_shape=pltpu.VMEM((256, COLS), F32), in_specs=[...  95.7 us

profile of v3, /device:TPU:193, one launch (start us, length us, event | category | flops | bytes accessed | tf_op | source)
XLA Modules:
  0.0 96.7 jit_solution(18294428528305192315)
XLA Ops:
  0.0 95.7 %shard_map.64 = f32[256,1024]{1,0:T(8,128)S(1)} custom-call(f32[256,1024]{1,0:T(8,128)} %bitcast.5, bf16[256,1024]{1,0:T(8,128)(2,1)} %bitcast.6, f32[128,1024]{1,0:T(8,128)} %bitcast.7, f32[2,128,128]{2,1,0:T(8,128)} %vinv_hbm.1, bf16[1024,256]{1,0:T(8,128)(2,1)} %w_in_hbm.1, bf16[256,1024]{1,0:T(8,128)(2,1)} %w_out_hbm.1), custom_call_target="tpu_custom_call" | custom-call | tf_op jit(solution)/shard_map/pallas_call | solution.py:299
  95.7 1.0 %copy.8 = f32[2,8,16,1024]{3,2,1,0:T(8,128)} copy(f32[2,8,16,1024]{3,2,1,0:T(8,128)S(1)} %bitcast.4) | data formatting | bytes 2097152

commit v4 on v3

--- a/solution.py
+++ b/solution.py
@@ -16,6 +16,7 @@
 LEVS = 16
 ROWS = 16
 HID = 1024
+AHEAD = 4
 TILES = COLS // 128
 
 
@@ -38,9 +39,9 @@
     state_hbm, cot_hbm, diff_hbm, vinv_hbm, w_in_hbm, w_out_hbm, out_hbm,
     state_v, cot_v, diff_v, vinv_v, w_in_v, w_out_v, out_v,
     cot_f, grid_s, grid_w, adj_v,
-    s_cot, r_cot, s_state, r_state, s_adj, r_adj,
+    s_edge, r_edge, s_cot, r_cot, s_state, r_state, s_adj, r_adj,
     w_in_p, w_in_t, w_out_t, v_fwd, v_adj, gain,
-    in_sems, tile_sems, cot_sems, state_sems, adj_sems, halo_a, halo_b,
+    in_sems, tile_sems, cot_sems, state_sems, adj_sems, edge_sems, pace,
 ):
     me = lax.axis_index("lev")
     hor = lax.axis_index("hor")
@@ -77,6 +78,17 @@
     def _():
         pl.semaphore_signal(barrier, inc=1, device_id={"lev": me, "hor": hor + 1}, device_id_type=MESH)
 
+    flipped = me + 2 - 4 * (lax.rem(me, 4) // 2)
+    stack = []
+    for step in (4, -4):
+        wraps = hor + step > last if step > 0 else hor + step < 0
+        stack.append({
+            "lev": jnp.where(wraps, flipped, me),
+            "hor": lax.rem(hor + step + last + 1, last + 1),
+        })
+    for neighbour in stack:
+        pl.semaphore_signal(barrier, inc=1, device_id=neighbour, device_id_type=MESH)
+
     def slot(r):
         depth = jnp.minimum(r, ROWS - 1 - r)
         return depth // 2, lax.rem(depth, 2) * 8 + (r >= ROWS // 2).astype(jnp.int32) * 4
@@ -116,8 +128,7 @@
     for load in state_load:
         load.wait()
 
-    @pl.loop(0, ROWS)
-    def _(r):
+    for r in (0, ROWS - 1):
         grid_s[r + 1] = both(state_v, r)
 
     @pl.when(hor == 0)
@@ -130,40 +141,40 @@
         grid_s[ROWS + 1] = jnp.zeros((16, COLS), F32)
         grid_w[ROWS + 1] = jnp.zeros((16, COLS), F32)
 
-    for load in rest:
-        load.wait()
-
     pl.semaphore_wait(
-        barrier, LEVS - 1 + (hor > 0).astype(jnp.int32) + (hor < last).astype(jnp.int32)
+        barrier, LEVS + 1 + (hor > 0).astype(jnp.int32) + (hor < last).astype(jnp.int32)
     )
 
-    def edge(grid, sems, up, cols):
-        src, dst = (ROWS, 0) if up else (1, ROWS + 1)
+    def edge(k, up):
         return pltpu.make_async_remote_copy(
-            src_ref=grid.at[src, :, cols], dst_ref=grid.at[dst, :, cols],
-            send_sem=sems.at[0, int(up)], recv_sem=sems.at[1, int(up)],
-            device_id={"lev": me, "hor": hor + (1 if up else -1)}, device_id_type=MESH,
+            src_ref=s_edge.at[k, up], dst_ref=r_edge.at[k, up],
+            send_sem=edge_sems.at[0, k, up], recv_sem=edge_sems.at[1, k, up],
+            device_id={"lev": me, "hor": hor + 2 * up - 1}, device_id_type=MESH,
         )
 
-    def swap_start(grid, sems, cols):
+    def swap_start(k, grid):
         @pl.when(hor > 0)
         def _():
-            edge(grid, sems, False, cols).start()
+            s_edge[k, 0] = grid[1].astype(BF16)
+            edge(k, 0).start()
 
         @pl.when(hor < last)
         def _():
-            edge(grid, sems, True, cols).start()
-
-    def swap_wait(grid, sems, cols):
+            s_edge[k, 1] = grid[ROWS].astype(BF16)
+            edge(k, 1).start()
+
+    def swap_wait(k, grid):
         @pl.when(hor > 0)
         def _():
-            edge(grid, sems, False, cols).wait_send()
-            edge(grid, sems, True, cols).wait_recv()
+            edge(k, 0).wait_send()
+            edge(k, 1).wait_recv()
+            grid[0] = r_edge[k, 1].astype(F32)
 
         @pl.when(hor < last)
         def _():
-            edge(grid, sems, True, cols).wait_send()
-            edge(grid, sems, False, cols).wait_recv()
+            edge(k, 1).wait_send()
+            edge(k, 0).wait_recv()
+            grid[ROWS + 1] = r_edge[k, 0].astype(F32)
 
     def spread(src, dst, sems, c):
         @pl.loop(1, LEVS)
@@ -179,23 +190,24 @@
         part = buf.at[c, pl.ds(0, LEVS - 1)]
         pltpu.make_async_copy(part, part, sems.at[way, c]).wait()
 
-    full = pl.ds(0, COLS)
-    swap_start(grid_s, halo_a, full)
+    swap_start(0, grid_s)
     for c in range(CHUNKS):
         spread(s_cot, r_cot, cot_sems, c)
 
-    swap_wait(grid_s, halo_a, full)
+    for load in rest:
+        load.wait()
+
+    @pl.loop(1, ROWS - 1)
+    def _(r):
+        grid_s[r + 1] = both(state_v, r)
+
+    swap_wait(0, grid_s)
 
     @pl.loop(0, ROWS)
     def _(r):
         mid = grid_s[r + 1]
         around = grid_s[r] + grid_s[r + 2] + sides_of(mid) - 4.0 * mid
         put(s_state, r, (mid + doubled(diff_v, r) * around).astype(BF16))
-
-    for c in range(CHUNKS):
-        spread(s_state, r_state, state_sems, c)
-    for c in range(CHUNKS):
-        r_state[c, me] = s_state[c, me]
 
     at_p = lax.broadcasted_iota(jnp.int32, (256, 256), 0)
     at_k = lax.broadcasted_iota(jnp.int32, (256, 256), 1)
@@ -225,6 +237,22 @@
     v_adj[:, 256:512] = high_t
     v_adj[:, 512:768] = parts[1].T.astype(BF16)
 
+    steps = [(s_cot, r_cot, cot_sems, c) for c in range(CHUNKS)]
+    steps += [(s_state, r_state, state_sems, c) for c in range(CHUNKS)]
+    for k in range(CHUNKS, len(steps)):
+        if k >= AHEAD:
+            before = steps[k - AHEAD]
+            gathered(before[1], before[2], 1, before[3])
+            for i, neighbour in enumerate(stack):
+                pl.semaphore_signal(pace.at[i], inc=1, device_id=neighbour, device_id_type=MESH)
+            for i in range(2):
+                pl.semaphore_wait(pace.at[i], 1)
+        spread(*steps[k])
+    done = len(steps) - AHEAD
+
+    for c in range(CHUNKS):
+        r_state[c, me] = s_state[c, me]
+
     def columns(c):
         diffused = r_state[c].reshape(256, WIDE)
         cot = r_cot[c].reshape(256, WIDE)
@@ -246,7 +274,10 @@
 
     @pl.loop(0, CHUNKS)
     def _(c):
-        gathered(r_cot, cot_sems, 1, c)
+        @pl.when(c >= done)
+        def _():
+            gathered(r_cot, cot_sems, 1, c)
+
         gathered(r_state, state_sems, 1, c)
         columns(c)
         spread(s_adj, r_adj, adj_sems, c)
@@ -276,9 +307,9 @@
         gathered(r_adj, adj_sems, 1, c)
         mirrored(2 * c, 2 * c + 2, weigh)
         if c == 0:
-            swap_start(grid_w, halo_b, full)
+            swap_start(1, grid_w)
         if c == CHUNKS - 2:
-            swap_wait(grid_w, halo_b, full)
+            swap_wait(1, grid_w)
             mirrored(0, 1, stencil)
         mirrored(max(1, 2 * c - 1), 2 * c + (2 if c == CHUNKS - 1 else 1), stencil)
 
@@ -307,10 +338,10 @@
             pltpu.VMEM((TILES, 256, 128), F32),
             pltpu.VMEM((TILES, 256, 128), F32), pltpu.VMEM((ROWS + 2, 16, COLS), F32),
             pltpu.VMEM((ROWS + 2, 16, COLS), F32), pltpu.VMEM((ROWS, 16, COLS), F32),
-        ] + [pltpu.VMEM(slabs, BF16)] * 6 + [
+        ] + [pltpu.VMEM((2, 2, 16, COLS), BF16)] * 2 + [pltpu.VMEM(slabs, BF16)] * 6 + [
             pltpu.VMEM((HID, 256), BF16), pltpu.VMEM((256, HID), BF16), pltpu.VMEM((HID, 256), BF16),
             pltpu.VMEM((256, 512), BF16), pltpu.VMEM((256, 768), BF16), pltpu.VMEM((256, 128), F32),
-            dma((4,)), dma((3, TILES)), dma((2, CHUNKS)), dma((2, CHUNKS)), dma((2, CHUNKS)), dma((2, 2)), dma((2, 2)),
+            dma((4,)), dma((3, TILES)), dma((2, CHUNKS)), dma((2, CHUNKS)), dma((2, CHUNKS)), dma((2, 2, 2)), pltpu.SemaphoreType.REGULAR((2,)),
         ],
         compiler_params=pltpu.CompilerParams(
             collective_id=0, has_side_effects=True, vmem_limit_bytes=44 << 20

time: 96.8 us -> 95.6 us (0.988)
  the two profiles are of different devices: /device:TPU:193 before, /device:TPU:121 now
where the time goes in v4:
time: 95.6 us; the launch traced here: 95.5 us
  Pallas kernels  94.5 us (99%)
  local copies, waits for them, and re-layouts  0.97 us (1%)
    pallas_call x1, Pallas kernels, body(): pl.pallas_call(kernel, out_shape=pltpu.VMEM((256, COLS), F32), in_specs=[...  94.5 us

profile of v4, /device:TPU:121, one launch (start us, length us, event | category | flops | bytes accessed | tf_op | source)
XLA Modules:
  0.0 95.5 jit_solution(17101322243200384508)
XLA Ops:
  0.0 94.5 %shard_map.64 = f32[256,1024]{1,0:T(8,128)S(1)} custom-call(f32[256,1024]{1,0:T(8,128)} %bitcast.5, bf16[256,1024]{1,0:T(8,128)(2,1)} %bitcast.6, f32[128,1024]{1,0:T(8,128)} %bitcast.7, f32[2,128,128]{2,1,0:T(8,128)} %vinv_hbm.1, bf16[1024,256]{1,0:T(8,128)(2,1)} %w_in_hbm.1, bf16[256,1024]{1,0:T(8,128)(2,1)} %w_out_hbm.1), custom_call_target="tpu_custom_call" | custom-call | tf_op jit(solution)/shard_map/pallas_call | solution.py:330
  94.5 1.0 %copy.8 = f32[2,8,16,1024]{3,2,1,0:T(8,128)} copy(f32[2,8,16,1024]{3,2,1,0:T(8,128)S(1)} %bitcast.4) | data formatting | bytes 2097152

commit v5 on v4

--- a/solution.py
+++ b/solution.py
@@ -41,7 +41,7 @@
     cot_f, grid_s, grid_w, adj_v,
     s_edge, r_edge, s_cot, r_cot, s_state, r_state, s_adj, r_adj,
     w_in_p, w_in_t, w_out_t, v_fwd, v_adj, gain,
-    in_sems, tile_sems, cot_sems, state_sems, adj_sems, edge_sems, pace,
+    in_sems, tile_sems, cot_sems, state_sems, adj_sems, edge_sems,
 ):
     me = lax.axis_index("lev")
     hor = lax.axis_index("hor")
@@ -78,17 +78,6 @@
     def _():
         pl.semaphore_signal(barrier, inc=1, device_id={"lev": me, "hor": hor + 1}, device_id_type=MESH)
 
-    flipped = me + 2 - 4 * (lax.rem(me, 4) // 2)
-    stack = []
-    for step in (4, -4):
-        wraps = hor + step > last if step > 0 else hor + step < 0
-        stack.append({
-            "lev": jnp.where(wraps, flipped, me),
-            "hor": lax.rem(hor + step + last + 1, last + 1),
-        })
-    for neighbour in stack:
-        pl.semaphore_signal(barrier, inc=1, device_id=neighbour, device_id_type=MESH)
-
     def slot(r):
         depth = jnp.minimum(r, ROWS - 1 - r)
         return depth // 2, lax.rem(depth, 2) * 8 + (r >= ROWS // 2).astype(jnp.int32) * 4
@@ -142,7 +131,7 @@
         grid_w[ROWS + 1] = jnp.zeros((16, COLS), F32)
 
     pl.semaphore_wait(
-        barrier, LEVS + 1 + (hor > 0).astype(jnp.int32) + (hor < last).astype(jnp.int32)
+        barrier, LEVS - 1 + (hor > 0).astype(jnp.int32) + (hor < last).astype(jnp.int32)
     )
 
     def edge(k, up):
@@ -243,10 +232,6 @@
         if k >= AHEAD:
             before = steps[k - AHEAD]
             gathered(before[1], before[2], 1, before[3])
-            for i, neighbour in enumerate(stack):
-                pl.semaphore_signal(pace.at[i], inc=1, device_id=neighbour, device_id_type=MESH)
-            for i in range(2):
-                pl.semaphore_wait(pace.at[i], 1)
         spread(*steps[k])
     done = len(steps) - AHEAD
 
@@ -341,7 +326,7 @@
         ] + [pltpu.VMEM((2, 2, 16, COLS), BF16)] * 2 + [pltpu.VMEM(slabs, BF16)] * 6 + [
             pltpu.VMEM((HID, 256), BF16), pltpu.VMEM((256, HID), BF16), pltpu.VMEM((HID, 256), BF16),
             pltpu.VMEM((256, 512), BF16), pltpu.VMEM((256, 768), BF16), pltpu.VMEM((256, 128), F32),
-            dma((4,)), dma((3, TILES)), dma((2, CHUNKS)), dma((2, CHUNKS)), dma((2, CHUNKS)), dma((2, 2, 2)), pltpu.SemaphoreType.REGULAR((2,)),
+            dma((4,)), dma((3, TILES)), dma((2, CHUNKS)), dma((2, CHUNKS)), dma((2, CHUNKS)), dma((2, 2, 2)),
         ],
         compiler_params=pltpu.CompilerParams(
             collective_id=0, has_side_effects=True, vmem_limit_bytes=44 << 20

time: 95.6 us -> 93.1 us (0.974)
  the two profiles are of different devices: /device:TPU:121 before, /device:TPU:65 now
where the time goes in v5:
time: 93.1 us; the launch traced here: 93 us
  Pallas kernels  92 us (99%)
  local copies, waits for them, and re-layouts  0.97 us (1%)
    pallas_call x1, Pallas kernels, body(): pl.pallas_call(kernel, out_shape=pltpu.VMEM((256, COLS), F32), in_specs=[...  92 us

profile of v5, /device:TPU:65, one launch (start us, length us, event | category | flops | bytes accessed | tf_op | source)
XLA Modules:
  0.0 93.0 jit_solution(1520353467579827730)
XLA Ops:
  0.0 92.0 %shard_map.64 = f32[256,1024]{1,0:T(8,128)S(1)} custom-call(f32[256,1024]{1,0:T(8,128)} %bitcast.5, bf16[256,1024]{1,0:T(8,128)(2,1)} %bitcast.6, f32[128,1024]{1,0:T(8,128)} %bitcast.7, f32[2,128,128]{2,1,0:T(8,128)} %vinv_hbm.1, bf16[1024,256]{1,0:T(8,128)(2,1)} %w_in_hbm.1, bf16[256,1024]{1,0:T(8,128)(2,1)} %w_out_hbm.1), custom_call_target="tpu_custom_call" | custom-call | tf_op jit(solution)/shard_map/pallas_call | solution.py:315
  92.0 1.0 %copy.8 = f32[2,8,16,1024]{3,2,1,0:T(8,128)} copy(f32[2,8,16,1024]{3,2,1,0:T(8,128)S(1)} %bitcast.4) | data formatting | bytes 2097152

commit v6 on v5

--- a/solution.py
+++ b/solution.py
@@ -16,7 +16,7 @@
 LEVS = 16
 ROWS = 16
 HID = 1024
-AHEAD = 4
+AHEAD = 3
 TILES = COLS // 128
 
 
@@ -228,6 +228,8 @@
 
     steps = [(s_cot, r_cot, cot_sems, c) for c in range(CHUNKS)]
     steps += [(s_state, r_state, state_sems, c) for c in range(CHUNKS)]
+    for k in range(CHUNKS - AHEAD):
+        gathered(steps[k][1], steps[k][2], 1, steps[k][3])
     for k in range(CHUNKS, len(steps)):
         if k >= AHEAD:
             before = steps[k - AHEAD]
@@ -263,7 +265,9 @@
         def _():
             gathered(r_cot, cot_sems, 1, c)
 
-        gathered(r_state, state_sems, 1, c)
+        @pl.when(c + CHUNKS >= done)
+        def _():
+            gathered(r_state, state_sems, 1, c)
         columns(c)
         spread(s_adj, r_adj, adj_sems, c)
         r_adj[c, me] = s_adj[c, me]

time: 93.1 us -> 99.1 us (1.064)
  the two profiles are of different devices: /device:TPU:65 before, /device:TPU:81 now
where the time goes in v6:
time: 99.1 us; the launch traced here: 99 us
  Pallas kernels  98 us (99%)
    pallas_call x1, Pallas kernels, body(): pl.pallas_call(kernel, out_shape=pltpu.VMEM((256, COLS), F32), in_specs=[...  98 us

profile of v6, /device:TPU:81, one launch (start us, length us, event | category | flops | bytes accessed | tf_op | source)
XLA Modules:
  0.0 99.0 jit_solution(17262327601290373240)
XLA Ops:
  0.0 98.0 %shard_map.64 = f32[256,1024]{1,0:T(8,128)S(1)} custom-call(f32[256,1024]{1,0:T(8,128)} %bitcast.5, bf16[256,1024]{1,0:T(8,128)(2,1)} %bitcast.6, f32[128,1024]{1,0:T(8,128)} %bitcast.7, f32[2,128,128]{2,1,0:T(8,128)} %vinv_hbm.1, bf16[1024,256]{1,0:T(8,128)(2,1)} %w_in_hbm.1, bf16[256,1024]{1,0:T(8,128)(2,1)} %w_out_hbm.1), custom_call_target="tpu_custom_call" | custom-call | tf_op jit(solution)/shard_map/pallas_call | solution.py:319
  98.0 1.0 copy.8
